TPU v7x, 512 devices: a whole 4x8x8 slice. The times are simulated.
512 devices in a mesh: stn: 16 (over z, core), chan: 32 (over y, x).
Axes of the slice: x: 4, y: 8, z: 8, core: 2. Of those that a mesh axis runs over, the one named last changes fastest.
Arguments:
- voltages: bfloat16 [256, 2048, 512], P('stn', 'chan'), may hold values from -6 to 6
- block_facet: int32 [32, 16, 2048, 1], P('chan', 'stn'), may hold values from 0 to 15; in each aligned block of 2048 rows (0 to 2047, 2048 to 4095, ..., all dimensions but the last counted through in order) at most 192 rows name the same one
- block_tile: int32 [32, 16, 2048], P('chan', 'stn'), may hold values from 0 to 15
- vis_offset: int32 [32, 16, 2048, 128], P('chan', 'stn'), may hold values from 0 to 624
- kernel_taps: bfloat16 [2, 8], replicated, may hold values from 0.19921875 to 1
Outputs:
- image: float32 [2, 2048, 128], P(None, ('stn', 'chan'))
Inputs may be any that keep to these rules, and one draw needn't show every extreme that they name: `block_facet`: among the blocks of one device (one index of the first two dimensions) at most 192 name one facet; in every draw some facet is named by exactly 192 of some device's blocks.
All inputs are finite; a program needn't handle non-finite values.
Results may differ from a plain program's by a relative error of at most 0.0041.
Values may be sent and summed in bfloat16 or wider, within the bound.
A program may use at most 64 MiB of HBM per device.

v0:
```python
import math
import jax
import jax.numpy as jnp
from jax import lax
from jax.sharding import PartitionSpec as P

VB = 128
TILE = 32
KT = 8
TS = 4
TT = 16
OFFS = 25


def kernel_rows(offsets, taps_row):
    cell_ids = jnp.arange(TILE, dtype=jnp.int32)
    distance = cell_ids[None, :, None] - offsets[:, None, :]
    weights_sum = jnp.zeros(distance.shape, jnp.float32)
    for tap_index in range(KT):
        weights_sum = weights_sum + jnp.where(
            distance == tap_index, taps_row[tap_index].astype(jnp.float32), jnp.float32(0.0)
        )
    return weights_sum.astype(jnp.bfloat16)


def block_tiles(values, offsets, kernel_taps):
    along_u = kernel_rows(offsets // OFFS, kernel_taps[0])
    along_v = kernel_rows(offsets % OFFS, kernel_taps[1])
    weighted = (
        values[:, :, None, :].astype(jnp.float32) * along_v[:, None, :, :].astype(jnp.float32)
    ).astype(jnp.bfloat16)
    weighted = weighted.reshape(values.shape[0], 2 * TILE, values.shape[2])
    return jnp.einsum("nux,nwx->nuw", along_u, weighted, preferred_element_type=jnp.float32)


def grid_blocks(values, offsets, target_ids, kernel_taps, segments):
    slot_count = values.shape[0]
    group_size = math.gcd(slot_count, 256)
    tile_width = 2 * TILE * TILE
    segment_ids = jnp.arange(segments, dtype=jnp.int32)

    def accumulate(grids, turn_index):
        first_row = turn_index * group_size
        part_values = lax.dynamic_slice_in_dim(values, first_row, group_size, 0)
        part_offsets = lax.dynamic_slice_in_dim(offsets, first_row, group_size, 0)
        part_targets = lax.dynamic_slice_in_dim(target_ids, first_row, group_size, 0)
        tile_sums = block_tiles(part_values, part_offsets, kernel_taps).reshape(
            group_size, tile_width
        )
        placing = (segment_ids[:, None] == part_targets[None, :]).astype(jnp.float32)
        grids = grids + jnp.dot(
            placing, tile_sums, precision=lax.Precision.HIGHEST, preferred_element_type=jnp.float32
        )
        return (grids, None)

    start_grids = jnp.zeros((segments, tile_width), jnp.float32)
    grids, leftover = lax.scan(accumulate, start_grids, jnp.arange(slot_count // group_size))
    return grids


def facet_grid(tile_grid):
    shaped = tile_grid.reshape(TS, TS, TILE, 2, TILE)
    return jnp.transpose(shaped, (3, 0, 2, 1, 4)).reshape(2, TS * TILE, TS * TILE)


def dft_tables(side):
    index_ids = jnp.arange(side, dtype=jnp.int32)
    phases = index_ids[:, None] * index_ids[None, :] % side
    angles = phases.astype(jnp.float32) * (2.0 * math.pi / side)
    return (jnp.cos(angles), jnp.sin(angles))


def column_pass(grid, cosine, sine):
    high = lax.Precision.HIGHEST
    real_cols = jnp.dot(grid[0], cosine, precision=high) + jnp.dot(grid[1], sine, precision=high)
    imag_cols = jnp.dot(grid[1], cosine, precision=high) - jnp.dot(grid[0], sine, precision=high)
    return (real_cols, imag_cols)


def row_pass(real_cols, imag_cols, cosine_rows, sine_rows):
    high = lax.Precision.HIGHEST
    real_rows = jnp.dot(cosine_rows, real_cols, precision=high) + jnp.dot(
        sine_rows, imag_cols, precision=high
    )
    imag_rows = jnp.dot(cosine_rows, imag_cols, precision=high) - jnp.dot(
        sine_rows, real_cols, precision=high
    )
    return (real_rows, imag_rows)


def body(voltages, block_facet, block_tile, vis_offset, kernel_taps):
    facets = lax.axis_size("stn")
    chan_count = lax.axis_size("chan")
    panels = lax.all_to_all(voltages, "stn", split_axis=1, concat_axis=0, tiled=True)
    stations = panels.shape[0]
    local_channels = panels.shape[1]
    samples = panels.shape[2] // 2
    swapped = jnp.concatenate([panels[:, :, samples:], -panels[:, :, :samples]], axis=2)
    stacked = jnp.concatenate([panels, swapped], axis=0)
    products = jnp.einsum("aks,jks->kaj", stacked, panels, preferred_element_type=jnp.float32)
    station_ids = jnp.arange(stations, dtype=jnp.int32)
    off_diagonal = (station_ids[:, None] != station_ids[None, :]).astype(jnp.float32)
    scale = 1.0 / math.sqrt(samples)
    real_vis = (products[:, :stations, :] * scale * off_diagonal).astype(jnp.bfloat16)
    imag_vis = (products[:, stations:, :] * scale * off_diagonal).astype(jnp.bfloat16)
    block_values = jnp.stack([real_vis.reshape(-1, VB), imag_vis.reshape(-1, VB)], axis=1)
    block_count = block_values.shape[0]
    offsets = vis_offset.reshape(block_count, VB)
    tile_ids = block_tile.reshape(block_count)
    facet_ids = block_facet.reshape(block_count)
    capacity = 3 * block_count // (2 * facets)
    facet_range = jnp.arange(facets, dtype=jnp.int32)
    member = (facet_ids[:, None] == facet_range[None, :]).astype(jnp.int32)
    earlier = jnp.cumsum(member, axis=0) - member
    position = jnp.sum(earlier * member, axis=1)
    slot_ids = facet_ids * capacity + position
    send_values = jnp.zeros((facets * capacity, 2, VB), jnp.bfloat16).at[slot_ids].set(block_values)
    send_offsets = jnp.zeros((facets * capacity, VB), jnp.int32).at[slot_ids].set(offsets)
    send_tiles = jnp.zeros((facets * capacity,), jnp.int32).at[slot_ids].set(tile_ids)
    got_values, got_offsets, got_tiles = (
        lax.all_to_all(send_values, "stn", split_axis=0, concat_axis=0, tiled=True),
        lax.all_to_all(send_offsets, "stn", split_axis=0, concat_axis=0, tiled=True),
        lax.all_to_all(send_tiles, "stn", split_axis=0, concat_axis=0, tiled=True),
    )
    tile_grid = grid_blocks(got_values, got_offsets, got_tiles, kernel_taps, TT)
    grid = facet_grid(tile_grid)
    side = grid.shape[1]
    row_count = side // chan_count
    channels_all = local_channels * facets * chan_count
    norm_factor = 1.0 / math.sqrt(channels_all * stations * stations * KT * KT / facets)
    cosine, sine = dft_tables(side)
    summed = lax.psum(grid, "chan")
    real_cols, imag_cols = column_pass(summed, cosine, sine)
    first_row = lax.axis_index("chan") * row_count
    cosine_rows = lax.dynamic_slice_in_dim(cosine, first_row, row_count, 0)
    sine_rows = lax.dynamic_slice_in_dim(sine, first_row, row_count, 0)
    real_rows, imag_rows = row_pass(real_cols, imag_cols, cosine_rows, sine_rows)
    image = jnp.stack([real_rows, imag_rows], axis=0) * norm_factor
    return image


def solution(mesh):
    placed = (
        P("stn", "chan", None),
        P("chan", "stn", None, None),
        P("chan", "stn", None),
        P("chan", "stn", None, None),
        P(),
    )
    return jax.shard_map(
        body, mesh=mesh, in_specs=placed, out_specs=P(None, ("stn", "chan"), None), check_vma=False
    )
```

profile of v0, /device:TPU:2, one launch (start us, length us, event | category | flops | bytes accessed | tf_op | source)
XLA Modules:
  0.0 876.2 jit_solution(455187938880387183)
XLA Ops:
  7.3 4.5 reduce-window.6
  14.1 8.2 scatter_custom_fusion
  23.0 10.4 %all-to-all-start = ((s32[16,192,1]{1,2,0:T(1,128)}), s32[16,192,1]{1,2,0:T(1,128)S(1)}, u32[]{:S(2)}, u32[]{:S(2)}) async-start(s32[16,192,1]{1,2,0:T(1,128)} %all_to_all.43), calls=%async_computation | async-start | bytes 32768 | tf_op jit(solution)/shard_map/all_to_all | solution.py:123
  36.2 4.9 all-to-all-done
  41.1 3.7 all-to-all-start.2
  44.7 6.8 scatter_custom_fusion.1
  51.6 19.8 %all-to-all-done.2 = bf16[16,64,512]{2,0,1:T(8,128)(2,1)S(1)} async-done(((bf16[16,64,512]{2,0,1:T(8,128)(2,1)}), bf16[16,64,512]{2,0,1:T(8,128)(2,1)S(1)}, u32[]{:S(2)}, u32[]{:S(2)}) %all-to-all-start.2) | async-done | bytes 1048608 | tf_op jit(solution)/shard_map/all_to_all | solution.py:94
  71.3 4.8 all-to-all-start.1
  84.7 185.7 %scatter_fusion = bf16[3072,2,128]{2,1,0:T(2,128)(2,1)} fusion(bf16[3072,2,128]{2,1,0:T(2,128)(2,1)} %broadcast_in_dim.128, s32[2048]{0:T(1024)S(1)} %bitcast.146, bf16[2048,2,128]{2,1,0:T(2,128)(2,1)S(1)} %pad_maximum_fusion), kind=kCustom, calls=%fused_computation.2 | custom fusion | bytes 3153920 | tf_op jit(solution)/shard_map/scatter | solution.py:117
  270.4 7.3 all-to-all-start.3
  278.0 37.6 %all-to-all-done.3 = bf16[3072,2,128]{2,1,0:T(2,128)(2,1)} async-done(((bf16[3072,2,128]{2,1,0:T(2,128)(2,1)}), bf16[3072,2,128]{2,1,0:T(2,128)(2,1)}, u32[]{:S(2)}, u32[]{:S(2)}) %all-to-all-start.3) | async-done | bytes 1572896 | tf_op jit(solution)/shard_map/all_to_all | solution.py:121
  315.6 394.3 %while.13 = (s32[]{:T(128)}, f32[16,2048]{1,0:T(8,128)S(1)}, s32[12]{0:T(128)S(1)}, s32[3072]{0:T(1024)S(1)}, s32[3072,128]{1,0:T(8,128)}, /*index=5*/bf16[2,8]{...) while((s32[]{:T(128)}, f32[16,2048]{1,0:T(8,128)S(1)}, ...), condition=%wide.region_7.8_spmd.clone, body=%wide.region_6.7_spmd.clone.sunk | while | flops 293081088 | bytes 26742172 | solution.py:57
  336.1 7.6 fusion.128
  343.7 3.5 copy.26
  368.9 7.6 fusion.128
  376.6 3.5 copy.26
  401.8 7.6 fusion.128
  409.4 3.5 copy.26
  434.6 7.6 fusion.128
  442.3 3.5 copy.26
  467.5 7.6 fusion.128
  475.1 3.5 copy.26
  500.3 7.6 fusion.128
  507.9 3.5 copy.26
  533.2 7.6 fusion.128
  566.0 7.6 fusion.128
  573.6 3.5 copy.26
  598.9 7.6 fusion.128
  631.7 7.6 fusion.128
  664.5 7.6 fusion.128
  697.4 7.6 fusion.128
  712.2 150.7 %all-reduce.2.cloned.1.call-done = f32[2,128,128]{2,1,0:T(8,128)} async-done(((f32[2,128,128]{2,1,0:T(8,128)}), f32[2,128,128]{2,1,0:T(8,128)}) %all-reduce.2.cloned.1.call-update) | async-done | bytes 131088 | tf_op jit(solution)/shard_map/psum | solution.py:132
  (143 shorter events, 173.9 us)
Async XLA Ops:
  6.5 38.2 %copy-start = (s32[1,1,2048,128]{3,2,1,0:T(8,128)S(1)}, s32[1,1,2048,128]{3,2,1,0:T(8,128)}, u32[]{:S(2)}) copy-start(s32[1,1,2048,128]{3,2,1,0:T(8,128)} %param.10) | copy-start | bytes 3145732
  23.0 18.1 %all-to-all-start = ((s32[16,192,1]{1,2,0:T(1,128)}), s32[16,192,1]{1,2,0:T(1,128)S(1)}, u32[]{:S(2)}, u32[]{:S(2)}) async-start(s32[16,192,1]{1,2,0:T(1,128)} %all_to_all.43), calls=%async_computation | async-start | bytes 32768 | tf_op jit(solution)/shard_map/all_to_all | solution.py:123
  41.1 30.3 %all-to-all-start.2 = ((bf16[16,64,512]{2,0,1:T(8,128)(2,1)}), bf16[16,64,512]{2,0,1:T(8,128)(2,1)S(1)}, u32[]{:S(2)}, u32[]{:S(2)}) async-start(bf16[16,64,512]{2,0,1:T(8,128)(2,1)} %copy.16), calls=%async_computation.2 | async-start | bytes 2097152 | tf_op jit(solution)/shard_map/all_to_all | solution.py:94
  71.3 199.0 %all-to-all-start.1 = ((s32[16,192,128]{2,1,0:T(8,128)}), s32[16,192,128]{2,1,0:T(8,128)}, u32[]{:S(2)}, u32[]{:S(2)}) async-start(s32[16,192,128]{2,1,0:T(8,128)} %bitcast.8), calls=%async_computation.1 | async-start | bytes 3145728 | tf_op jit(solution)/shard_map/all_to_all | solution.py:122
  82.5 233.0 %copy-start.1 = (bf16[2,8]{1,0:T(2,128)(2,1)S(1)}, bf16[2,8]{1,0:T(2,128)(2,1)}, u32[]{:S(2)}) copy-start(bf16[2,8]{1,0:T(2,128)(2,1)} %param.11) | copy-start | bytes 100
  270.4 45.2 %all-to-all-start.3 = ((bf16[3072,2,128]{2,1,0:T(2,128)(2,1)}), bf16[3072,2,128]{2,1,0:T(2,128)(2,1)}, u32[]{:S(2)}, u32[]{:S(2)}) async-start(bf16[3072,2,128]{2,1,0:T(2,128)(2,1)} %scatter_fusion), calls=%async_computation.3 | async-start | bytes 3145728 | tf_op jit(solution)/shard_map/all_to_all | solution.py:121
  277.6 585.3 %all-reduce.2.cloned.1.call-start = ((), (), s32[]{:S(2)}) async-start(), calls=%async_computation.4 | async-start | bytes 262144 | tf_op jit(solution)/shard_map/psum | solution.py:132
Sparse Core Ops, SparseCore 0:
  711.7 151.1 all-reduce.1
where the time goes:
time: 881 us; the launch traced here: 876 us
  local copies, waits for them, and re-layouts  271 us (31%)
  waiting for transfers between devices  213 us (24%)
  loops' own time  128 us (15%)
  other arithmetic  114 us (13%)
  matrix products  111 us (13%)
  starting transfers between devices  26.4 us (3%)
  between operations  13.6 us (2%)
    scatter x1, local copies, waits for them, and re-layouts, body(): jnp.zeros((facets * capacity, 2, VB), jnp.bfloat16).at[slot_ids]  186 us
    psum x1, waiting for transfers between devices, body(): summed = lax.psum(grid, 'chan')  151 us
    another operation x1, loops' own time, grid_blocks(): lax.scan(accumulate, start_grids, jnp.arange(slot_count // group_size))  128 us
    dot_general x12, matrix products, block_tiles(): jnp.einsum('nux,nwx->nuw', along_u, weighted, preferred_element_type=jnp....  91.5 us
    dot_general x12, local copies, waits for them, and re-layouts, block_tiles(): jnp.einsum('nux,nwx->nuw', along_u, weighted, preferred_element_type=jnp....  42.5 us
    convert_element_type x12, other arithmetic, block_tiles(): along_v[:, None, :, :].astype(jnp.float32)  38.9 us
    convert_element_type x12, other arithmetic, block_tiles(): weighted = (values[:, :, None, :].astype(jnp.float32) * along_v[:, None,...  38.3 us
    all_to_all x1, waiting for transfers between devices, body(): lax.all_to_all(send_values, 'stn', split_axis=0, concat_axis=0, tiled=True)  37.6 us
  transfers between devices with their start and end apart: 5, of which 4 were waited for; matrix products, arithmetic and copies ran while one was open for 23% of the time, Pallas kernels for 0%

commit v1 on v0

--- a/solution.py
+++ b/solution.py
@@ -129,7 +129,7 @@
     channels_all = local_channels * facets * chan_count
     norm_factor = 1.0 / math.sqrt(channels_all * stations * stations * KT * KT / facets)
     cosine, sine = dft_tables(side)
-    summed = lax.psum(grid, "chan")
+    summed = jnp.sum(jax.lax.all_gather(grid, "chan"), 0)
     real_cols, imag_cols = column_pass(summed, cosine, sine)
     first_row = lax.axis_index("chan") * row_count
     cosine_rows = lax.dynamic_slice_in_dim(cosine, first_row, row_count, 0)

time: 881 us -> 815 us (0.925)
  the two profiles are of different devices: /device:TPU:2 before, /device:TPU:8 now
where the time goes in v1:
time: 815 us; the launch traced here: 811 us
  local copies, waits for them, and re-layouts  271 us (33%)
  waiting for transfers between devices  148 us (18%)
  loops' own time  128 us (16%)
  other arithmetic  116 us (14%)
  matrix products  107 us (13%)
  starting transfers between devices  26.8 us (3%)
  between operations  13.6 us (2%)
    scatter x1, local copies, waits for them, and re-layouts, body(): jnp.zeros((facets * capacity, 2, VB), jnp.bfloat16).at[slot_ids]  186 us
    another operation x1, loops' own time, grid_blocks(): lax.scan(accumulate, start_grids, jnp.arange(slot_count // group_size))  128 us
    dot_general x12, matrix products, block_tiles(): jnp.einsum('nux,nwx->nuw', along_u, weighted, preferred_element_type=jnp....  91.5 us
    all_gather x1, waiting for transfers between devices, body(): summed = jnp.sum(jax.lax.all_gather(grid, 'chan'), 0)  85.6 us
    dot_general x12, local copies, waits for them, and re-layouts, block_tiles(): jnp.einsum('nux,nwx->nuw', along_u, weighted, preferred_element_type=jnp....  42.5 us
    convert_element_type x12, other arithmetic, block_tiles(): along_v[:, None, :, :].astype(jnp.float32)  38.9 us
    convert_element_type x12, other arithmetic, block_tiles(): weighted = (values[:, :, None, :].astype(jnp.float32) * along_v[:, None,...  38.3 us
    all_to_all x1, waiting for transfers between devices, body(): lax.all_to_all(send_values, 'stn', split_axis=0, concat_axis=0, tiled=True)  37.6 us
  transfers between devices with their start and end apart: 5, of which 4 were waited for; matrix products, arithmetic and copies ran while one was open for 25% of the time, Pallas kernels for 0%

profile of v1, /device:TPU:8, one launch (start us, length us, event | category | flops | bytes accessed | tf_op | source)
XLA Modules:
  0.0 810.6 jit_solution(1468969592821285502)
XLA Ops:
  7.3 4.5 reduce-window.6
  14.1 8.2 %scatter_custom_fusion = s32[3072]{0:T(1024)S(1)} fusion(s32[2048]{0:T(1024)S(1)} %bitcast.144, s32[2048]{0:T(1024)} %bitcast.149, s32[]{:T(128)} %constant.120.clone.1), kind=kCustom, calls=%fused_computation.113 | custom fusion | bytes 12800 | tf_op jit(solution)/shard_map/scatter | solution.py:119
  23.0 10.4 %all-to-all-start = ((s32[16,192,1]{1,2,0:T(1,128)}), s32[16,192,1]{1,2,0:T(1,128)S(1)}, u32[]{:S(2)}, u32[]{:S(2)}) async-start(s32[16,192,1]{1,2,0:T(1,128)} %all_to_all.43), calls=%async_computation | async-start | bytes 32768 | tf_op jit(solution)/shard_map/all_to_all | solution.py:123
  36.2 4.9 all-to-all-done
  41.1 3.7 all-to-all-start.2
  44.7 6.8 scatter_custom_fusion.1
  51.6 19.8 %all-to-all-done.2 = bf16[16,64,512]{2,0,1:T(8,128)(2,1)S(1)} async-done(((bf16[16,64,512]{2,0,1:T(8,128)(2,1)}), bf16[16,64,512]{2,0,1:T(8,128)(2,1)S(1)}, u32[]{:S(2)}, u32[]{:S(2)}) %all-to-all-start.2) | async-done | bytes 1048608 | tf_op jit(solution)/shard_map/all_to_all | solution.py:94
  71.3 4.8 all-to-all-start.1
  84.7 185.6 %scatter_fusion = bf16[3072,2,128]{2,1,0:T(2,128)(2,1)} fusion(bf16[3072,2,128]{2,1,0:T(2,128)(2,1)} %broadcast_in_dim.128, s32[2048]{0:T(1024)S(1)} %bitcast.146, bf16[2048,2,128]{2,1,0:T(2,128)(2,1)S(1)} %pad_maximum_fusion), kind=kCustom, calls=%fused_computation.2 | custom fusion | bytes 3153920 | tf_op jit(solution)/shard_map/scatter | solution.py:117
  270.3 7.8 all-to-all-start.3
  278.5 37.6 %all-to-all-done.3 = bf16[3072,2,128]{2,1,0:T(2,128)(2,1)} async-done(((bf16[3072,2,128]{2,1,0:T(2,128)(2,1)}), bf16[3072,2,128]{2,1,0:T(2,128)(2,1)}, u32[]{:S(2)}, u32[]{:S(2)}) %all-to-all-start.3) | async-done | bytes 1572896 | tf_op jit(solution)/shard_map/all_to_all | solution.py:121
  316.0 394.4 %while.13 = (s32[]{:T(128)}, f32[16,2048]{1,0:T(8,128)S(1)}, s32[12]{0:T(128)S(1)}, s32[3072]{0:T(1024)S(1)}, s32[3072,128]{1,0:T(8,128)}, /*index=5*/bf16[2,8]{...) while((s32[]{:T(128)}, f32[16,2048]{1,0:T(8,128)S(1)}, ...), condition=%wide.region_7.8_spmd.clone, body=%wide.region_6.7_spmd.clone.sunk | while | flops 293081088 | bytes 26742172 | solution.py:57
  336.5 7.6 fusion.128
  344.2 3.5 copy.26
  369.4 7.6 fusion.128
  377.0 3.5 copy.26
  402.2 7.6 fusion.128
  409.9 3.5 copy.26
  435.1 7.6 fusion.128
  442.7 3.5 copy.26
  467.9 7.6 fusion.128
  500.8 7.6 fusion.128
  533.6 7.6 fusion.128
  541.3 3.5 copy.26
  566.5 7.6 fusion.128
  599.3 7.6 fusion.128
  607.0 3.5 copy.26
  632.2 7.6 fusion.128
  665.0 7.6 fusion.128
  697.9 7.6 fusion.128
  705.5 3.5 copy.26
  712.6 85.6 %all-gather.2.cloned.1.call-done = f32[32,2,128,128]{3,2,1,0:T(8,128)} async-done(((f32[1,2,128,128]{3,2,1,0:T(8,128)}), f32[32,2,128,128]{3,2,1,0:T(8,128)}) %all-gather.2.cloned.1.call-update) | async-done | bytes 4194320 | tf_op jit(solution)/shard_map/all_gather | solution.py:132
  (144 shorter events, 173.0 us)
Async XLA Ops:
  6.5 38.2 %copy-start = (s32[1,1,2048,128]{3,2,1,0:T(8,128)S(1)}, s32[1,1,2048,128]{3,2,1,0:T(8,128)}, u32[]{:S(2)}) copy-start(s32[1,1,2048,128]{3,2,1,0:T(8,128)} %param.10) | copy-start | bytes 3145732
  23.0 18.1 %all-to-all-start = ((s32[16,192,1]{1,2,0:T(1,128)}), s32[16,192,1]{1,2,0:T(1,128)S(1)}, u32[]{:S(2)}, u32[]{:S(2)}) async-start(s32[16,192,1]{1,2,0:T(1,128)} %all_to_all.43), calls=%async_computation | async-start | bytes 32768 | tf_op jit(solution)/shard_map/all_to_all | solution.py:123
  41.1 30.3 %all-to-all-start.2 = ((bf16[16,64,512]{2,0,1:T(8,128)(2,1)}), bf16[16,64,512]{2,0,1:T(8,128)(2,1)S(1)}, u32[]{:S(2)}, u32[]{:S(2)}) async-start(bf16[16,64,512]{2,0,1:T(8,128)(2,1)} %copy.16), calls=%async_computation.2 | async-start | bytes 2097152 | tf_op jit(solution)/shard_map/all_to_all | solution.py:94
  71.3 199.0 %all-to-all-start.1 = ((s32[16,192,128]{2,1,0:T(8,128)}), s32[16,192,128]{2,1,0:T(8,128)}, u32[]{:S(2)}, u32[]{:S(2)}) async-start(s32[16,192,128]{2,1,0:T(8,128)} %bitcast.8), calls=%async_computation.1 | async-start | bytes 3145728 | tf_op jit(solution)/shard_map/all_to_all | solution.py:122
  82.5 233.5 %copy-start.1 = (bf16[2,8]{1,0:T(2,128)(2,1)S(1)}, bf16[2,8]{1,0:T(2,128)(2,1)}, u32[]{:S(2)}) copy-start(bf16[2,8]{1,0:T(2,128)(2,1)} %param.11) | copy-start | bytes 100
  270.3 45.7 %all-to-all-start.3 = ((bf16[3072,2,128]{2,1,0:T(2,128)(2,1)}), bf16[3072,2,128]{2,1,0:T(2,128)(2,1)}, u32[]{:S(2)}, u32[]{:S(2)}) async-start(bf16[3072,2,128]{2,1,0:T(2,128)(2,1)} %scatter_fusion), calls=%async_computation.3 | async-start | bytes 3145728 | tf_op jit(solution)/shard_map/all_to_all | solution.py:121
  278.1 520.1 %all-gather.2.cloned.1.call-start = ((), (), s32[]{:S(2)}) async-start(), calls=%async_computation.4 | async-start | bytes 4325376 | tf_op jit(solution)/shard_map/all_gather | solution.py:132
Sparse Core Ops, SparseCore 0:
  712.2 85.9 all-gather.1
